TPU v7x, 128 devices: a whole 4x4x4 slice. The times are simulated.
128 devices in a mesh: lat: 8 (over x, y_hi), lon: 16 (over z, y_lo, core).
Axes of the slice: x: 4, y: 4 (y_hi: 2, y_lo: 2; y = y_hi * 2 + y_lo), z: 4, core: 2. Of those that a mesh axis runs over, the one named last changes fastest.
Arguments:
- features: bfloat16 [256, 384, 2048], P('lat', 'lon'), may hold values from -6 to 6
- atrous_weight: bfloat16 [3, 3, 2048, 256], replicated, may hold values from -0.046875 to 0.046875
- norm_gain: float32 [256], replicated, may hold values from 0.1 to 1.9
- norm_bias: float32 [256], replicated, may hold values from -0.5 to 0.5
- head_weight: float32 [3, 256], replicated, may hold values from -1.5 to 1.5
- labels: int32 [256, 384], P('lat', 'lon'), may hold values from 0 to 2
Outputs:
- mean_loss: float32 [], replicated
- grad_features: bfloat16 [256, 384, 2048], P('lat', 'lon')
- grad_weight: float32 [2048, 3, 3, 256], P('lat', None, None, 'lon')
- grad_gain: float32 [256], replicated
- grad_bias: float32 [256], replicated
- grad_head: float32 [3, 256], replicated
All inputs are finite; a program needn't handle non-finite values.
Results may differ from a plain program's by a relative error of at most 0.022.
Values may be sent and summed in bfloat16 or wider, within the bound.
No kernel may reach another device: no remote copies, remote signals or barrier semaphores. Data moves between devices by JAX's collectives and lax.ppermute only.
A program may use at most 192 MiB of HBM per device.

v0:
```python
import jax
import jax.numpy as jnp
from jax import lax
from jax.sharding import PartitionSpec as P

RATE = 12
epsilon = 1e-05


def padded_2(block, sides, width, periodic):
    for axis, dim in sides:
        count = lax.axis_size(axis)
        forward = [(i, i + 1) for i in range(count - 1)]
        if periodic:
            forward.append((count - 1, 0))
        backward = [(target, source) for source, target in forward]
        low = lax.ppermute(
            lax.slice_in_dim(block, block.shape[dim] - width, None, axis=dim), axis, forward
        )
        high = lax.ppermute(lax.slice_in_dim(block, 0, width, axis=dim), axis, backward)
        block = jnp.concatenate([low, block, high], axis=dim)
    return block


def shards(features, atrous_weight, norm_gain, norm_bias, head_weight, labels):
    height, breadth, channels = features.shape
    filters = atrous_weight.shape[3]
    local_cells = height * breadth
    total_cells = local_cells * lax.axis_size("lat") * lax.axis_size("lon")
    flat_input = features.reshape(local_cells, channels)
    lon_padded = padded_2(features, (("lon", 1),), RATE, True)
    padded = padded_2(lon_padded, (("lat", 0),), RATE, False)
    summed = jnp.zeros((local_cells, filters), jnp.float32)
    for tap_row in range(3):
        for tap_col in range(3):
            window = padded[
                tap_row * RATE : tap_row * RATE + height, tap_col * RATE : tap_col * RATE + breadth
            ]
            summed = summed + jnp.dot(
                window.reshape(local_cells, channels),
                atrous_weight[tap_row, tap_col],
                preferred_element_type=jnp.float32,
            )
    moments = lax.psum((jnp.sum(summed, 0), jnp.sum(summed * summed, 0)), ("lat", "lon"))
    average = moments[0] / total_cells
    variance = moments[1] / total_cells - average * average
    inverse = lax.rsqrt(variance + epsilon)
    normed = (summed - average) * inverse
    preact = norm_gain * normed + norm_bias
    hidden = jnp.maximum(preact, 0.0).astype(jnp.bfloat16)
    hidden_wide = hidden.astype(jnp.float32)
    logits = jnp.dot(hidden_wide, head_weight.T, precision=lax.Precision.HIGHEST)
    one_hot = (
        labels.reshape(local_cells)[:, None]
        == jnp.arange(head_weight.shape[0], dtype=jnp.int32)[None, :]
    ).astype(jnp.float32)
    exponent = jnp.exp(logits)
    partition = jnp.sum(exponent, 1, keepdims=True)
    loss_terms = jnp.sum(jnp.log(partition)[:, 0] - jnp.sum(logits * one_hot, 1))
    grad_logits = exponent / partition - one_hot
    head_term = jnp.dot(grad_logits.T, hidden_wide, precision=lax.Precision.HIGHEST)
    d_hidden = jnp.dot(grad_logits, head_weight, precision=lax.Precision.HIGHEST)
    d_preact = jnp.where(preact > 0, d_hidden, 0.0)
    totals = lax.psum(
        (jnp.sum(d_preact, 0), jnp.sum(d_preact * normed, 0), head_term, loss_terms), ("lat", "lon")
    )
    grad_bias = totals[0] / total_cells
    grad_gain = totals[1] / total_cells
    grad_head = totals[2] / total_cells
    mean_loss = totals[3] / total_cells
    d_summed = (norm_gain * inverse * (d_preact - grad_bias - normed * grad_gain)).astype(
        jnp.bfloat16
    )
    d_grid = d_summed.reshape(height, breadth, filters)
    grad_lon = padded_2(d_grid, (("lon", 1),), RATE, True)
    grad_padded = padded_2(grad_lon, (("lat", 0),), RATE, False)
    grad_acc = jnp.zeros((local_cells, channels), jnp.float32)
    shifted_taps = []
    for tap_row in range(3):
        for tap_col in range(3):
            row_first = (2 - tap_row) * RATE
            col_first = (2 - tap_col) * RATE
            shifted = grad_padded[
                row_first : row_first + height, col_first : col_first + breadth
            ].reshape(local_cells, filters)
            shifted_taps.append(shifted)
            grad_acc = grad_acc + lax.dot_general(
                shifted,
                atrous_weight[tap_row, tap_col],
                (((1,), (1,)), ((), ())),
                preferred_element_type=jnp.float32,
            )
    grad_features = grad_acc.astype(jnp.bfloat16).reshape(height, breadth, channels)
    channel_block = channels // lax.axis_size("lat")
    filter_block = filters // lax.axis_size("lon")
    shifted_all = jnp.stack(shifted_taps, 0)
    lon_summed = lax.psum_scatter(
        jnp.einsum(
            "tqf,qc->ftc", shifted_all, flat_input, preferred_element_type=jnp.float32
        ).astype(jnp.bfloat16),
        "lon",
        scatter_dimension=0,
        tiled=True,
    )
    weight_block = jnp.transpose(
        lax.psum_scatter(lon_summed, "lat", scatter_dimension=2, tiled=True).astype(jnp.float32),
        (2, 1, 0),
    )
    grad_weight = (weight_block / total_cells).reshape(channel_block, 3, 3, filter_block)
    return (mean_loss, grad_features, grad_weight, grad_gain, grad_bias, grad_head)


def solution(mesh):
    return jax.shard_map(
        shards,
        mesh=mesh,
        in_specs=(P("lat", "lon", None), P(), P(), P(), P(), P("lat", "lon")),
        out_specs=(P(), P("lat", "lon", None), P("lat", None, None, "lon"), P(), P(), P()),
        check_vma=False,
    )
```

profile of v0, /device:TPU:0, one launch (start us, length us, event | category | flops | bytes accessed | tf_op | source)
XLA Modules:
  0.0 566.8 jit_solution(16156541013725347236)
XLA Ops:
  7.2 3.1 fusion.63
  11.2 4.6 collective-permute-start.1
  16.8 31.3 %collective-permute-done.1 = bf16[32,12,2048]{2,0,1:T(8,128)(2,1)S(1)} collective-permute-done((bf16[32,12,2048]{2,0,1:T(8,128)(2,1)S(1)}, bf16[32,12,2048]{2,0,1:T(8,128)(2,1)S(1)}, u32[]{:S(2)}, u32[]{:S(2)}) %collective-permute-start.1) | collective-permute-done | bytes 1572896 | tf_op jit(solution)/shard_map/ppermute | solution.py:20
  52.6 4.8 pad_maximum_fusion.5
  57.4 6.4 %collective-permute-start.2 = (bf16[12,48,2048]{2,1,0:T(8,128)(2,1)}, bf16[12,48,2048]{2,1,0:T(8,128)(2,1)}, u32[]{:S(2)}, u32[]{:S(2)}) collective-permute-start(bf16[12,48,2048]{2,1,0:T(8,128)(2,1)} %get-tuple-element.26), channel_id=1, source_target_pairs={{0,16},{16,32},{32,48},{48,64},{64,80},{80,96},{96,112},{1,17},{17... | collective-permute-start | bytes 7077896 | tf_op jit(solution)/shard_map/ppermute | solution.py:17
  67.9 4.2 pad_maximum_fusion.1
  72.0 3.1 fusion.26
  75.1 83.8 %collective-permute-done.2 = bf16[12,48,2048]{2,1,0:T(8,128)(2,1)} collective-permute-done((bf16[12,48,2048]{2,1,0:T(8,128)(2,1)}, bf16[12,48,2048]{2,1,0:T(8,128)(2,1)}, u32[]{:S(2)}, u32[]{:S(2)}) %collective-permute-start.2) | collective-permute-done | bytes 2359328 | tf_op jit(solution)/shard_map/ppermute | solution.py:17
  158.9 10.6 %maximum_maximum_fusion = (bf16[44,48,2048]{2,1,0:T(8,128)(2,1)S(1)}, bf16[44,48,2048]{2,1,0:T(8,128)(2,1)}) fusion(bf16[32,12,2048]{2,1,0:T(8,128)(2,1)S(1)} %copy-done.4, bf16[32,24,2048]{2,1,0:T(8,128)(2,1)S(1)} %copy-done.2, bf16[32,12,2048]{2,1,0:T(8,128)(2,1)S(1)} %copy-done.6, bf16[12,48,2048]{2,1,0:T(8,128)(2,1)} %collective-permute-done.2, ...), kind=kLoop, calls=%fused_computation.1 | loop fusion | flops 69206016 | bytes 28311552 | tf_op jit(solution)/shard_map/concatenate | solution.py:21
  169.5 10.5 %fusion.61 = (bf16[32,24,2048]{2,1,0:T(8,128)(2,1)}, bf16[32,24,2048]{2,1,0:T(8,128)(2,1)}, bf16[32,24,2048]{2,1,0:T(8,128)(2,1)}, bf16[32,24,2048]{2,1,0:T(8,12...) fusion(bf16[44,48,2048]{2,1,0:T(8,128)(2,1)S(1)} %get-tuple-element.24, ...), kind=kLoop, calls=%fused_computation.106 | loop fusion | bytes 37748736 | tf_op jit(solution)/shard_map/slice | solution.py:36
  180.0 3.3 fusion.30
  195.4 3.1 fusion.60
  198.5 70.8 %all-reduce.1 = (f32[256]{0:T(256)S(1)}, f32[256]{0:T(256)S(1)}) all-reduce(f32[256]{0:T(256)S(1)} %get-tuple-element.9, f32[256]{0:T(256)S(1)} %get-tuple-element.8), channel_id=1, replica_groups=mesh['lat'=8,'lon'=16] {'lat','lon'}, use_global_device_ids=true, to_apply=%region_3.0 | all-reduce | flops 512 | bytes 4096 | tf_op jit(solution)/shard_map/psum | solution.py:44
  271.9 3.0 fusion.59
  275.6 62.6 %all-reduce = (f32[]{:T(128)}, f32[256]{0:T(256)S(1)}, f32[256]{0:T(256)S(1)}, f32[3,256]{1,0:T(4,128)}) all-reduce(f32[]{:T(128)} %subtract_reduce_fusion, f32[256]{0:T(256)S(1)} %get-tuple-element.7, f32[256]{0:T(256)S(1)} %get-tuple-element.6, f32[3,256]{1,0:T(4,128)S(1)} %fusion.58), channel_id=1, replica_groups=mesh['lat'=8,'lon'=16] {'lat','lon'}, use_global_device_ids=true, to_apply=%region_7.8 | all-reduce | flops 1281 | bytes 10248 | tf_op jit(solution)/shard_map/psum | solution.py:64
  339.9 3.8 collective-permute-start.5
  343.7 6.5 %collective-permute-done.4 = bf16[32,12,256]{2,1,0:T(8,128)(2,1)S(1)} collective-permute-done((bf16[32,12,256]{2,1,0:T(8,128)(2,1)S(1)}, bf16[32,12,256]{2,1,0:T(8,128)(2,1)S(1)}, u32[]{:S(2)}, u32[]{:S(2)}) %collective-permute-start.4) | collective-permute-done | bytes 196640 | tf_op jit(solution)/shard_map/ppermute | solution.py:17
  351.7 6.1 %collective-permute-start.7 = (bf16[12,48,256]{2,1,0:T(8,128)(2,1)S(1)}, bf16[12,48,256]{2,1,0:T(8,128)(2,1)S(1)}, u32[]{:S(2)}, u32[]{:S(2)}) collective-permute-start(bf16[12,48,256]{2,1,0:T(8,128)(2,1)S(1)} %get-tuple-element.41), channel_id=1, source_target_pairs={{0,16},{16,32},{32,48},{48,64},{64,80},{80,96},{96,112},{1,17},{17... | collective-permute-start | bytes 884744 | tf_op jit(solution)/shard_map/ppermute | solution.py:17
  358.2 3.5 collective-permute-done.6
  361.7 4.8 collective-permute-done.7
  368.4 9.8 %convert_bitcast_fusion = bf16[256,9,2048]{2,0,1:T(8,128)(2,1)} fusion(bf16[9,768,256]{2,1,0:T(8,128)(2,1)S(1)} %bitcast_dynamic-update-slice_fusion, bf16[768,2048,1]{1,0,2:T(8,128)(2,1)S(1)} %bitcast.124), kind=kOutput, calls=%fused_computation | convolution fusion | flops 7252475904 | bytes 16121856 | tf_op jit(solution)/shard_map/tqf,qc->ftc/dot_general | solution.py:98
  379.8 5.1 fusion.20
  384.9 5.0 fusion.17
  389.9 3.7 fusion.24
  393.6 3.6 fusion.13
  397.2 3.6 fusion.9
  400.8 3.7 fusion.36
  404.5 3.6 fusion.28
  408.1 3.6 fusion.32
  411.8 75.0 %reduce-scatter.3.cloned.1.call-done = bf16[16,9,2048]{2,0,1:T(8,128)(2,1)} async-done(((bf16[256,9,2048]{2,0,1:T(8,128)(2,1)}), bf16[16,9,2048]{2,0,1:T(8,128)(2,1)}) %reduce-scatter.3.cloned.1.call-update) | async-done | bytes 589840 | tf_op jit(solution)/shard_map/reduce_scatter | solution.py:97
  486.8 18.9 %add_convert_fusion = bf16[768,2048]{1,0:T(8,128)(2,1)} fusion(f32[768,2048]{1,0:T(8,128)} %fusion.9, f32[768,2048]{1,0:T(8,128)} %fusion.13, f32[768,2048]{1,0:T(8,128)} %fusion.17, f32[768,2048]{1,0:T(8,128)} %fusion.20, f32[768,2048]{1,0:T(8,128)} %fusion.24, f32[768,2048]{1,0:T(8,128)} %fusion.28, f32[768,2048]{1,0:T(8,128)} %fusion.36, ...), kind=kOutput, calls=%fused_computation.3 | convolution fusion | flops 819462144 | bytes 54919168 | tf_op jit(solution)/shard_map/dot_general | solution.py:87
  505.7 51.4 %reduce-scatter.5.cloned.1.call-done = bf16[16,9,256]{2,0,1:T(8,128)(2,1)} async-done(((bf16[16,9,2048]{2,0,1:T(8,128)(2,1)}), bf16[16,9,256]{2,0,1:T(8,128)(2,1)}) %reduce-scatter.5.cloned.1.call-update) | async-done | bytes 73744 | tf_op jit(solution)/shard_map/reduce_scatter | solution.py:106
  (127 shorter events, 33.1 us)
Async XLA Ops:
  7.2 264.0 %copy-start = (f32[3,256]{1,0:T(4,128)S(1)}, f32[3,256]{1,0:T(4,128)}, u32[]{:S(2)}) copy-start(f32[3,256]{1,0:T(4,128)} %param.10) | copy-start | bytes 9220
  7.2 479.5 %reduce-scatter.3.cloned.1.call-start = ((), (), s32[]{:S(2)}) async-start(), calls=%async_computation.2 | async-start | bytes 10027008 | tf_op jit(solution)/shard_map/reduce_scatter | solution.py:97
  11.2 36.9 %collective-permute-start.1 = (bf16[32,12,2048]{2,0,1:T(8,128)(2,1)S(1)}, bf16[32,12,2048]{2,0,1:T(8,128)(2,1)S(1)}, u32[]{:S(2)}, u32[]{:S(2)}) collective-permute-start(bf16[32,12,2048]{2,0,1:T(8,128)(2,1)S(1)} %copy.25), channel_id=1, source_target_pairs={{1,0},{2,1},{3,2},{4,3},{5,4},{6,5},{7,6},{8,7},{9,8},{10,9},{11,1... | collective-permute-start | bytes 4718600 | tf_op jit(solution)/shard_map/ppermute | solution.py:20
  16.7 35.8 %copy-start.2 = (bf16[32,24,2048]{2,1,0:T(8,128)(2,1)S(1)}, bf16[32,24,2048]{2,1,0:T(8,128)(2,1)}, u32[]{:S(2)}) copy-start(bf16[32,24,2048]{2,1,0:T(8,128)(2,1)} %param.6) | copy-start | bytes 9437188
  16.7 34.9 %collective-permute-start = (bf16[32,12,2048]{2,0,1:T(8,128)(2,1)S(1)}, bf16[32,12,2048]{2,0,1:T(8,128)(2,1)S(1)}, u32[]{:S(2)}, u32[]{:S(2)}) collective-permute-start(bf16[32,12,2048]{2,0,1:T(8,128)(2,1)S(1)} %copy.24), channel_id=1, source_target_pairs={{0,1},{1,2},{2,3},{3,4},{4,5},{5,6},{6,7},{7,8},{8,9},{9,10},{10,1... | collective-permute-start | bytes 4718600 | tf_op jit(solution)/shard_map/ppermute | solution.py:17
  49.0 8.4 %copy-start.3 = (bf16[32,12,2048]{2,1,0:T(8,128)(2,1)}, bf16[32,12,2048]{2,1,0:T(8,128)(2,1)S(1)}, u32[]{:S(2)}) copy-start(bf16[32,12,2048]{2,1,0:T(8,128)(2,1)S(1)} %copy.18) | copy-start | bytes 4718596
  52.6 4.9 copy-start.5
  52.6 12.6 %copy-start.30 = (s32[32,24]{0,1:T(8,128)S(1)}, s32[32,24]{0,1:T(8,128)}, u32[]{:S(2)}) copy-start(s32[32,24]{0,1:T(8,128)} %param.11) | copy-start | bytes 9220
  57.4 101.4 %collective-permute-start.2 = (bf16[12,48,2048]{2,1,0:T(8,128)(2,1)}, bf16[12,48,2048]{2,1,0:T(8,128)(2,1)}, u32[]{:S(2)}, u32[]{:S(2)}) collective-permute-start(bf16[12,48,2048]{2,1,0:T(8,128)(2,1)} %get-tuple-element.26), channel_id=1, source_target_pairs={{0,16},{16,32},{32,48},{48,64},{64,80},{80,96},{96,112},{1,17},{17... | collective-permute-start | bytes 7077896 | tf_op jit(solution)/shard_map/ppermute | solution.py:17
  63.9 95.0 %collective-permute-start.3 = (bf16[12,48,2048]{2,1,0:T(8,128)(2,1)}, bf16[12,48,2048]{2,1,0:T(8,128)(2,1)}, u32[]{:S(2)}, u32[]{:S(2)}) collective-permute-start(bf16[12,48,2048]{2,1,0:T(8,128)(2,1)} %get-tuple-element.27), channel_id=1, source_target_pairs={{16,0},{32,16},{48,32},{64,48},{80,64},{96,80},{112,96},{17,1},{33... | collective-permute-start | bytes 7077896 | tf_op jit(solution)/shard_map/ppermute | solution.py:20
  195.4 73.9 %copy-start.33 = (f32[256]{0:T(256)S(1)}, f32[256]{0:T(256)}, u32[]{:S(2)}) copy-start(f32[256]{0:T(256)} %param.8) | copy-start | bytes 3076
  195.4 74.5 %copy-start.35 = (f32[256]{0:T(256)S(1)}, f32[256]{0:T(256)}, u32[]{:S(2)}) copy-start(f32[256]{0:T(256)} %param.9) | copy-start | bytes 3076
  338.1 28.7 %copy-start.31 = (f32[256]{0:T(256)}, f32[256]{0:T(256)S(1)}, u32[]{:S(2)}) copy-start(f32[256]{0:T(256)S(1)} %broadcast_multiply_fusion.1) | copy-start | bytes 3076
  338.1 28.7 %copy-start.32 = (f32[256]{0:T(256)}, f32[256]{0:T(256)S(1)}, u32[]{:S(2)}) copy-start(f32[256]{0:T(256)S(1)} %broadcast_multiply_fusion.2) | copy-start | bytes 3076
  339.8 10.4 %collective-permute-start.4 = (bf16[32,12,256]{2,1,0:T(8,128)(2,1)S(1)}, bf16[32,12,256]{2,1,0:T(8,128)(2,1)S(1)}, u32[]{:S(2)}, u32[]{:S(2)}) collective-permute-start(bf16[32,12,256]{2,1,0:T(8,128)(2,1)S(1)} %get-tuple-element.44), channel_id=1, source_target_pairs={{0,1},{1,2},{2,3},{3,4},{4,5},{5,6},{6,7},{7,8},{8,9},{9,10},{10,1... | collective-permute-start | bytes 589832 | tf_op jit(solution)/shard_map/ppermute | solution.py:17
  339.9 10.4 %collective-permute-start.5 = (bf16[32,12,256]{2,1,0:T(8,128)(2,1)S(1)}, bf16[32,12,256]{2,1,0:T(8,128)(2,1)S(1)}, u32[]{:S(2)}, u32[]{:S(2)}) collective-permute-start(bf16[32,12,256]{2,1,0:T(8,128)(2,1)S(1)} %get-tuple-element.45), channel_id=1, source_target_pairs={{1,0},{2,1},{3,2},{4,3},{5,4},{6,5},{7,6},{8,7},{9,8},{10,9},{11,1... | collective-permute-start | bytes 589832 | tf_op jit(solution)/shard_map/ppermute | solution.py:20
  350.4 11.2 %collective-permute-start.6 = (bf16[12,48,256]{2,1,0:T(8,128)(2,1)S(1)}, bf16[12,48,256]{2,1,0:T(8,128)(2,1)S(1)}, u32[]{:S(2)}, u32[]{:S(2)}) collective-permute-start(bf16[12,48,256]{2,1,0:T(8,128)(2,1)S(1)} %get-tuple-element.40), channel_id=1, source_target_pairs={{16,0},{32,16},{48,32},{64,48},{80,64},{96,80},{112,96},{17,1},{33... | collective-permute-start | bytes 884744 | tf_op jit(solution)/shard_map/ppermute | solution.py:20
  351.7 14.7 %collective-permute-start.7 = (bf16[12,48,256]{2,1,0:T(8,128)(2,1)S(1)}, bf16[12,48,256]{2,1,0:T(8,128)(2,1)S(1)}, u32[]{:S(2)}, u32[]{:S(2)}) collective-permute-start(bf16[12,48,256]{2,1,0:T(8,128)(2,1)S(1)} %get-tuple-element.41), channel_id=1, source_target_pairs={{0,16},{16,32},{32,48},{48,64},{64,80},{80,96},{96,112},{1,17},{17... | collective-permute-start | bytes 884744 | tf_op jit(solution)/shard_map/ppermute | solution.py:17
  358.1 9.3 %copy-start.19 = (bf16[32,24,256]{2,1,0:T(8,128)(2,1)}, bf16[32,24,256]{2,1,0:T(8,128)(2,1)S(1)}, u32[]{:S(2)}) copy-start(bf16[32,24,256]{2,1,0:T(8,128)(2,1)S(1)} %get-tuple-element.42) | copy-start | bytes 1179652
  358.1 9.4 %copy-start.21 = (bf16[32,24,256]{2,1,0:T(8,128)(2,1)}, bf16[32,24,256]{2,1,0:T(8,128)(2,1)S(1)}, u32[]{:S(2)}) copy-start(bf16[32,24,256]{2,1,0:T(8,128)(2,1)S(1)} %get-tuple-element.43) | copy-start | bytes 1179652
  378.3 178.7 %reduce-scatter.5.cloned.1.call-start = ((), (), s32[]{:S(2)}) async-start(), calls=%async_computation.3 | async-start | bytes 663552 | tf_op jit(solution)/shard_map/reduce_scatter | solution.py:106
  379.8 5.1 copy-start.22
  379.8 10.0 %slice-start = ((s8[9437184]{0:T(1024)(128)(4,1)}), s8[4194304]{0:T(1024)(128)(4,1)S(1)}, s32[]{:S(2)}) async-start(s8[9437184]{0:T(1024)(128)(4,1)} %bitcast.131), calls=%async_computation.4 | async-start | bytes 8388608
  379.8 10.0 %slice-start.1 = ((s8[9437184]{0:T(1024)(128)(4,1)}), s8[4194304]{0:T(1024)(128)(4,1)S(1)}, s32[]{:S(2)}) async-start(s8[9437184]{0:T(1024)(128)(4,1)} %bitcast.131), calls=%async_computation.5 | async-start | bytes 8388608
  384.9 5.0 slice-start.2
  384.9 5.0 copy-start.20
  389.9 3.7 copy-start.18
  397.2 3.6 copy-start.14
  400.8 3.7 copy-start.12
  404.5 3.6 copy-start.10
  408.1 78.6 %copy-start.24 = (bf16[32,24,256]{2,1,0:T(8,128)(2,1)S(1)}, bf16[32,24,256]{2,1,0:T(8,128)(2,1)}, u32[]{:S(2)}) copy-start(bf16[32,24,256]{2,1,0:T(8,128)(2,1)} %copy-done.23) | copy-start | bytes 1179652
  486.8 71.8 %copy-start.1 = (f32[3,256]{1,0:T(4,128)S(1)}, f32[3,256]{1,0:T(4,128)}, u32[]{:S(2)}) copy-start(f32[3,256]{1,0:T(4,128)} %param.10) | copy-start | bytes 9220
  (17 other events, 32.8 us)
Sparse Core Ops, SparseCore 0:
  378.4 108.2 reduce-scatter.2
  490.3 66.6 reduce-scatter.4
where the time goes:
time: 574 us; the launch traced here: 567 us
  waiting for transfers between devices  259 us (45%)
  blocking collectives  133 us (23%)
  matrix products  88.1 us (15%)
  other arithmetic  26.7 us (5%)
  starting transfers between devices  24 us (4%)
  local copies, waits for them, and re-layouts  19.1 us (3%)
  between operations  16.7 us (3%)
    ppermute x4, waiting for transfers between devices, padded_2(): lax.ppermute(lax.slice_in_dim(block, block.shape[dim] - width, None, axis...  97.7 us
    reduce_scatter x1, waiting for transfers between devices, shards(): lax.psum_scatter(jnp.einsum('tqf,qc->ftc', shifted_all, flat_input, prefe...  75 us
    psum x1, blocking collectives, shards(): lax.psum((jnp.sum(summed, 0), jnp.sum(summed * summed, 0)), ('lat', 'lon'))  70.8 us
    psum x1, blocking collectives, shards(): lax.psum((jnp.sum(d_preact, 0), jnp.sum(d_preact * normed, 0), head_term,...  62.6 us
    reduce_scatter x1, waiting for transfers between devices, shards(): lax.psum_scatter(lon_summed, 'lat', scatter_dimension=2, tiled=True)  51.4 us
    dot_general x9, matrix products, shards(): lax.dot_general(shifted, atrous_weight[tap_row, tap_col], (((1,), (1,)),...  50.8 us
    ppermute x4, waiting for transfers between devices, padded_2(): lax.ppermute(lax.slice_in_dim(block, 0, width, axis=dim), axis, backward)  34.8 us
    dot_general x9, matrix products, shards(): jnp.dot(window.reshape(local_cells, channels), atrous_weight[tap_row, tap...  23.8 us
  transfers between devices with their start and end apart: 10, of which 8 were waited for; matrix products, arithmetic and copies ran while one was open for 11% of the time, Pallas kernels for 0%

commit v1 on v0

--- a/solution.py
+++ b/solution.py
@@ -5,6 +5,12 @@
 
 RATE = 12
 epsilon = 1e-05
+
+
+def sites_search(t0):
+    for ix in ("lat", "lon"):
+        t0 = lax.psum(t0, axis_name=ix)
+    return t0
 
 
 def padded_2(block, sides, width, periodic):
@@ -41,7 +47,7 @@
                 atrous_weight[tap_row, tap_col],
                 preferred_element_type=jnp.float32,
             )
-    moments = lax.psum((jnp.sum(summed, 0), jnp.sum(summed * summed, 0)), ("lat", "lon"))
+    moments = sites_search((jnp.sum(summed, 0), jnp.sum(summed * summed, 0)))
     average = moments[0] / total_cells
     variance = moments[1] / total_cells - average * average
     inverse = lax.rsqrt(variance + epsilon)

time: 574 us -> 555 us (0.967)
  blocking collectives: 133 us -> 115 us
    psum x1 -> x2, blocking collectives: 70.8 us -> 52.7 us  [sites_search(): t0 = lax.psum(t0, axis_name=ix)]
  transfers between devices with their start and end apart: 10 -> 10, of which waited for: 8 -> 8; matrix products, arithmetic and copies ran while one was open for 11% -> 12% of each run, Pallas kernels for 0% -> 0%
where the time goes in v1:
time: 555 us; the launch traced here: 549 us
  waiting for transfers between devices  259 us (47%)
  blocking collectives  115 us (21%)
  matrix products  88.2 us (16%)
  other arithmetic  26.7 us (5%)
  starting transfers between devices  24 us (4%)
  local copies, waits for them, and re-layouts  19.2 us (3%)
  between operations  16.7 us (3%)
    ppermute x4, waiting for transfers between devices, padded_2(): lax.ppermute(lax.slice_in_dim(block, block.shape[dim] - width, None, axis...  97.7 us
    reduce_scatter x1, waiting for transfers between devices, shards(): lax.psum_scatter(jnp.einsum('tqf,qc->ftc', shifted_all, flat_input, prefe...  74.3 us
    psum x1, blocking collectives, shards(): lax.psum((jnp.sum(d_preact, 0), jnp.sum(d_preact * normed, 0), head_term,...  62.4 us
    psum x2, blocking collectives, sites_search(): t0 = lax.psum(t0, axis_name=ix)  52.7 us
    reduce_scatter x1, waiting for transfers between devices, shards(): lax.psum_scatter(lon_summed, 'lat', scatter_dimension=2, tiled=True)  51.4 us
    dot_general x9, matrix products, shards(): lax.dot_general(shifted, atrous_weight[tap_row, tap_col], (((1,), (1,)),...  50.8 us
    ppermute x4, waiting for transfers between devices, padded_2(): lax.ppermute(lax.slice_in_dim(block, 0, width, axis=dim), axis, backward)  35.3 us
    dot_general x9, matrix products, shards(): jnp.dot(window.reshape(local_cells, channels), atrous_weight[tap_row, tap...  23.8 us
  transfers between devices with their start and end apart: 10, of which 8 were waited for; matrix products, arithmetic and copies ran while one was open for 12% of the time, Pallas kernels for 0%

profile of v1, /device:TPU:0, one launch (start us, length us, event | category | flops | bytes accessed | tf_op | source)
XLA Modules:
  0.0 548.6 jit_solution(12151367167659939716)
XLA Ops:
  7.2 3.1 fusion.63
  11.2 4.6 collective-permute-start.1
  16.8 31.3 %collective-permute-done.1 = bf16[32,12,2048]{2,0,1:T(8,128)(2,1)S(1)} collective-permute-done((bf16[32,12,2048]{2,0,1:T(8,128)(2,1)S(1)}, bf16[32,12,2048]{2,0,1:T(8,128)(2,1)S(1)}, u32[]{:S(2)}, u32[]{:S(2)}) %collective-permute-start.1) | collective-permute-done | bytes 1572896 | tf_op jit(solution)/shard_map/ppermute | solution.py:26
  52.6 4.8 pad_maximum_fusion.5
  57.4 6.4 %collective-permute-start.2 = (bf16[12,48,2048]{2,1,0:T(8,128)(2,1)}, bf16[12,48,2048]{2,1,0:T(8,128)(2,1)}, u32[]{:S(2)}, u32[]{:S(2)}) collective-permute-start(bf16[12,48,2048]{2,1,0:T(8,128)(2,1)} %get-tuple-element.28), channel_id=1, source_target_pairs={{0,16},{16,32},{32,48},{48,64},{64,80},{80,96},{96,112},{1,17},{17... | collective-permute-start | bytes 7077896 | tf_op jit(solution)/shard_map/ppermute | solution.py:23
  67.9 4.2 pad_maximum_fusion.1
  72.0 3.1 fusion.26
  75.1 83.8 %collective-permute-done.2 = bf16[12,48,2048]{2,1,0:T(8,128)(2,1)} collective-permute-done((bf16[12,48,2048]{2,1,0:T(8,128)(2,1)}, bf16[12,48,2048]{2,1,0:T(8,128)(2,1)}, u32[]{:S(2)}, u32[]{:S(2)}) %collective-permute-start.2) | collective-permute-done | bytes 2359328 | tf_op jit(solution)/shard_map/ppermute | solution.py:23
  158.9 10.6 %maximum_maximum_fusion = (bf16[44,48,2048]{2,1,0:T(8,128)(2,1)S(1)}, bf16[44,48,2048]{2,1,0:T(8,128)(2,1)}) fusion(bf16[32,12,2048]{2,1,0:T(8,128)(2,1)S(1)} %copy-done.4, bf16[32,24,2048]{2,1,0:T(8,128)(2,1)S(1)} %copy-done.2, bf16[32,12,2048]{2,1,0:T(8,128)(2,1)S(1)} %copy-done.6, bf16[12,48,2048]{2,1,0:T(8,128)(2,1)} %collective-permute-done.2, ...), kind=kLoop, calls=%fused_computation.1 | loop fusion | flops 69206016 | bytes 28311552 | tf_op jit(solution)/shard_map/concatenate | solution.py:27
  169.5 10.6 %fusion.61 = (bf16[32,24,2048]{2,1,0:T(8,128)(2,1)}, bf16[32,24,2048]{2,1,0:T(8,128)(2,1)}, bf16[32,24,2048]{2,1,0:T(8,128)(2,1)}, bf16[32,24,2048]{2,1,0:T(8,12...) fusion(bf16[44,48,2048]{2,1,0:T(8,128)(2,1)S(1)} %get-tuple-element.26, ...), kind=kLoop, calls=%fused_computation.106 | loop fusion | bytes 37748736 | tf_op jit(solution)/shard_map/slice | solution.py:42
  180.1 3.3 fusion.30
  195.5 3.1 fusion.60
  198.6 23.3 %all-reduce.2 = (f32[256]{0:T(256)S(1)}, f32[256]{0:T(256)S(1)}) all-reduce(f32[256]{0:T(256)S(1)} %get-tuple-element.9, f32[256]{0:T(256)S(1)} %get-tuple-element.8), channel_id=1, replica_groups=mesh['lat'=8,'lon'=16] {'lat'}, use_global_device_ids=true, to_apply=%region_4.0 | all-reduce | flops 512 | bytes 4096 | tf_op jit(solution)/shard_map/psum | solution.py:12
  221.9 29.4 %all-reduce.1 = (f32[256]{0:T(256)S(1)}, f32[256]{0:T(256)S(1)}) all-reduce(f32[256]{0:T(256)S(1)} %get-tuple-element.18, f32[256]{0:T(256)S(1)} %get-tuple-element.19), channel_id=1, replica_groups=mesh['lat'=8,'lon'=16] {'lon'}, use_global_device_ids=true, to_apply=%region_5.0 | all-reduce | flops 512 | bytes 4096 | tf_op jit(solution)/shard_map/psum | solution.py:12
  257.6 62.4 %all-reduce = (f32[]{:T(128)}, f32[256]{0:T(256)S(1)}, f32[256]{0:T(256)S(1)}, f32[3,256]{1,0:T(4,128)}) all-reduce(f32[]{:T(128)} %subtract_reduce_fusion, f32[256]{0:T(256)S(1)} %get-tuple-element.7, f32[256]{0:T(256)S(1)} %get-tuple-element.6, f32[3,256]{1,0:T(4,128)S(1)} %fusion.58), channel_id=1, replica_groups=mesh['lat'=8,'lon'=16] {'lat','lon'}, use_global_device_ids=true, to_apply=%region_9.10 | all-reduce | flops 1281 | bytes 10248 | tf_op jit(solution)/shard_map/psum | solution.py:70
  321.8 3.8 collective-permute-start.5
  325.7 6.7 %collective-permute-done.4 = bf16[32,12,256]{2,1,0:T(8,128)(2,1)S(1)} collective-permute-done((bf16[32,12,256]{2,1,0:T(8,128)(2,1)S(1)}, bf16[32,12,256]{2,1,0:T(8,128)(2,1)S(1)}, u32[]{:S(2)}, u32[]{:S(2)}) %collective-permute-start.4) | collective-permute-done | bytes 196640 | tf_op jit(solution)/shard_map/ppermute | solution.py:23
  333.8 6.1 %collective-permute-start.7 = (bf16[12,48,256]{2,1,0:T(8,128)(2,1)S(1)}, bf16[12,48,256]{2,1,0:T(8,128)(2,1)S(1)}, u32[]{:S(2)}, u32[]{:S(2)}) collective-permute-start(bf16[12,48,256]{2,1,0:T(8,128)(2,1)S(1)} %get-tuple-element.43), channel_id=1, source_target_pairs={{0,16},{16,32},{32,48},{48,64},{64,80},{80,96},{96,112},{1,17},{17... | collective-permute-start | bytes 884744 | tf_op jit(solution)/shard_map/ppermute | solution.py:23
  340.2 4.0 collective-permute-done.6
  344.2 4.6 collective-permute-done.7
  350.8 9.8 %convert_bitcast_fusion = bf16[256,9,2048]{2,0,1:T(8,128)(2,1)} fusion(bf16[9,768,256]{2,1,0:T(8,128)(2,1)S(1)} %bitcast_dynamic-update-slice_fusion, bf16[768,2048,1]{1,0,2:T(8,128)(2,1)S(1)} %bitcast.124), kind=kOutput, calls=%fused_computation | convolution fusion | flops 7252475904 | bytes 16121856 | tf_op jit(solution)/shard_map/tqf,qc->ftc/dot_general | solution.py:104
  362.2 5.1 fusion.20
  367.2 5.0 fusion.17
  372.3 3.7 fusion.24
  376.0 3.6 fusion.13
  379.6 3.6 fusion.9
  383.2 3.7 fusion.36
  386.9 3.6 fusion.28
  390.6 3.6 fusion.32
  394.2 74.3 %reduce-scatter.3.cloned.1.call-done = bf16[16,9,2048]{2,0,1:T(8,128)(2,1)} async-done(((bf16[256,9,2048]{2,0,1:T(8,128)(2,1)}), bf16[16,9,2048]{2,0,1:T(8,128)(2,1)}) %reduce-scatter.3.cloned.1.call-update) | async-done | bytes 589840 | tf_op jit(solution)/shard_map/reduce_scatter | solution.py:103
  468.6 18.9 %add_convert_fusion = bf16[768,2048]{1,0:T(8,128)(2,1)} fusion(f32[768,2048]{1,0:T(8,128)} %fusion.9, f32[768,2048]{1,0:T(8,128)} %fusion.13, f32[768,2048]{1,0:T(8,128)} %fusion.17, f32[768,2048]{1,0:T(8,128)} %fusion.20, f32[768,2048]{1,0:T(8,128)} %fusion.24, f32[768,2048]{1,0:T(8,128)} %fusion.28, f32[768,2048]{1,0:T(8,128)} %fusion.36, ...), kind=kOutput, calls=%fused_computation.3 | convolution fusion | flops 819462144 | bytes 54919168 | tf_op jit(solution)/shard_map/dot_general | solution.py:93
  487.5 51.4 %reduce-scatter.5.cloned.1.call-done = bf16[16,9,256]{2,0,1:T(8,128)(2,1)} async-done(((bf16[16,9,2048]{2,0,1:T(8,128)(2,1)}), bf16[16,9,256]{2,0,1:T(8,128)(2,1)}) %reduce-scatter.5.cloned.1.call-update) | async-done | bytes 73744 | tf_op jit(solution)/shard_map/reduce_scatter | solution.py:112
  (128 shorter events, 36.2 us)
Async XLA Ops:
  7.2 246.0 %copy-start = (f32[3,256]{1,0:T(4,128)S(1)}, f32[3,256]{1,0:T(4,128)}, u32[]{:S(2)}) copy-start(f32[3,256]{1,0:T(4,128)} %param.10) | copy-start | bytes 9220
  7.2 461.3 %reduce-scatter.3.cloned.1.call-start = ((), (), s32[]{:S(2)}) async-start(), calls=%async_computation.2 | async-start | bytes 10027008 | tf_op jit(solution)/shard_map/reduce_scatter | solution.py:103
  11.2 36.9 %collective-permute-start.1 = (bf16[32,12,2048]{2,0,1:T(8,128)(2,1)S(1)}, bf16[32,12,2048]{2,0,1:T(8,128)(2,1)S(1)}, u32[]{:S(2)}, u32[]{:S(2)}) collective-permute-start(bf16[32,12,2048]{2,0,1:T(8,128)(2,1)S(1)} %copy.25), channel_id=1, source_target_pairs={{1,0},{2,1},{3,2},{4,3},{5,4},{6,5},{7,6},{8,7},{9,8},{10,9},{11,1... | collective-permute-start | bytes 4718600 | tf_op jit(solution)/shard_map/ppermute | solution.py:26
  16.7 35.8 %copy-start.2 = (bf16[32,24,2048]{2,1,0:T(8,128)(2,1)S(1)}, bf16[32,24,2048]{2,1,0:T(8,128)(2,1)}, u32[]{:S(2)}) copy-start(bf16[32,24,2048]{2,1,0:T(8,128)(2,1)} %param.6) | copy-start | bytes 9437188
  16.7 34.9 %collective-permute-start = (bf16[32,12,2048]{2,0,1:T(8,128)(2,1)S(1)}, bf16[32,12,2048]{2,0,1:T(8,128)(2,1)S(1)}, u32[]{:S(2)}, u32[]{:S(2)}) collective-permute-start(bf16[32,12,2048]{2,0,1:T(8,128)(2,1)S(1)} %copy.24), channel_id=1, source_target_pairs={{0,1},{1,2},{2,3},{3,4},{4,5},{5,6},{6,7},{7,8},{8,9},{9,10},{10,1... | collective-permute-start | bytes 4718600 | tf_op jit(solution)/shard_map/ppermute | solution.py:23
  49.0 8.4 %copy-start.3 = (bf16[32,12,2048]{2,1,0:T(8,128)(2,1)}, bf16[32,12,2048]{2,1,0:T(8,128)(2,1)S(1)}, u32[]{:S(2)}) copy-start(bf16[32,12,2048]{2,1,0:T(8,128)(2,1)S(1)} %copy.18) | copy-start | bytes 4718596
  52.6 4.9 copy-start.5
  52.6 12.6 %copy-start.30 = (s32[32,24]{0,1:T(8,128)S(1)}, s32[32,24]{0,1:T(8,128)}, u32[]{:S(2)}) copy-start(s32[32,24]{0,1:T(8,128)} %param.11) | copy-start | bytes 9220
  57.4 101.4 %collective-permute-start.2 = (bf16[12,48,2048]{2,1,0:T(8,128)(2,1)}, bf16[12,48,2048]{2,1,0:T(8,128)(2,1)}, u32[]{:S(2)}, u32[]{:S(2)}) collective-permute-start(bf16[12,48,2048]{2,1,0:T(8,128)(2,1)} %get-tuple-element.28), channel_id=1, source_target_pairs={{0,16},{16,32},{32,48},{48,64},{64,80},{80,96},{96,112},{1,17},{17... | collective-permute-start | bytes 7077896 | tf_op jit(solution)/shard_map/ppermute | solution.py:23
  63.9 95.0 %collective-permute-start.3 = (bf16[12,48,2048]{2,1,0:T(8,128)(2,1)}, bf16[12,48,2048]{2,1,0:T(8,128)(2,1)}, u32[]{:S(2)}, u32[]{:S(2)}) collective-permute-start(bf16[12,48,2048]{2,1,0:T(8,128)(2,1)} %get-tuple-element.29), channel_id=1, source_target_pairs={{16,0},{32,16},{48,32},{64,48},{80,64},{96,80},{112,96},{17,1},{33... | collective-permute-start | bytes 7077896 | tf_op jit(solution)/shard_map/ppermute | solution.py:26
  195.5 55.9 %copy-start.33 = (f32[256]{0:T(256)S(1)}, f32[256]{0:T(256)}, u32[]{:S(2)}) copy-start(f32[256]{0:T(256)} %param.8) | copy-start | bytes 3076
  195.5 56.4 %copy-start.35 = (f32[256]{0:T(256)S(1)}, f32[256]{0:T(256)}, u32[]{:S(2)}) copy-start(f32[256]{0:T(256)} %param.9) | copy-start | bytes 3076
  320.0 29.1 %copy-start.31 = (f32[256]{0:T(256)}, f32[256]{0:T(256)S(1)}, u32[]{:S(2)}) copy-start(f32[256]{0:T(256)S(1)} %broadcast_multiply_fusion.1) | copy-start | bytes 3076
  320.1 29.1 %copy-start.32 = (f32[256]{0:T(256)}, f32[256]{0:T(256)S(1)}, u32[]{:S(2)}) copy-start(f32[256]{0:T(256)S(1)} %broadcast_multiply_fusion.2) | copy-start | bytes 3076
  321.7 10.6 %collective-permute-start.4 = (bf16[32,12,256]{2,1,0:T(8,128)(2,1)S(1)}, bf16[32,12,256]{2,1,0:T(8,128)(2,1)S(1)}, u32[]{:S(2)}, u32[]{:S(2)}) collective-permute-start(bf16[32,12,256]{2,1,0:T(8,128)(2,1)S(1)} %get-tuple-element.46), channel_id=1, source_target_pairs={{0,1},{1,2},{2,3},{3,4},{4,5},{5,6},{6,7},{7,8},{8,9},{9,10},{10,1... | collective-permute-start | bytes 589832 | tf_op jit(solution)/shard_map/ppermute | solution.py:23
  321.8 10.5 %collective-permute-start.5 = (bf16[32,12,256]{2,1,0:T(8,128)(2,1)S(1)}, bf16[32,12,256]{2,1,0:T(8,128)(2,1)S(1)}, u32[]{:S(2)}, u32[]{:S(2)}) collective-permute-start(bf16[32,12,256]{2,1,0:T(8,128)(2,1)S(1)} %get-tuple-element.47), channel_id=1, source_target_pairs={{1,0},{2,1},{3,2},{4,3},{5,4},{6,5},{7,6},{8,7},{9,8},{10,9},{11,1... | collective-permute-start | bytes 589832 | tf_op jit(solution)/shard_map/ppermute | solution.py:26
  332.5 11.7 %collective-permute-start.6 = (bf16[12,48,256]{2,1,0:T(8,128)(2,1)S(1)}, bf16[12,48,256]{2,1,0:T(8,128)(2,1)S(1)}, u32[]{:S(2)}, u32[]{:S(2)}) collective-permute-start(bf16[12,48,256]{2,1,0:T(8,128)(2,1)S(1)} %get-tuple-element.42), channel_id=1, source_target_pairs={{16,0},{32,16},{48,32},{64,48},{80,64},{96,80},{112,96},{17,1},{33... | collective-permute-start | bytes 884744 | tf_op jit(solution)/shard_map/ppermute | solution.py:26
  333.8 15.0 %collective-permute-start.7 = (bf16[12,48,256]{2,1,0:T(8,128)(2,1)S(1)}, bf16[12,48,256]{2,1,0:T(8,128)(2,1)S(1)}, u32[]{:S(2)}, u32[]{:S(2)}) collective-permute-start(bf16[12,48,256]{2,1,0:T(8,128)(2,1)S(1)} %get-tuple-element.43), channel_id=1, source_target_pairs={{0,16},{16,32},{32,48},{48,64},{64,80},{80,96},{96,112},{1,17},{17... | collective-permute-start | bytes 884744 | tf_op jit(solution)/shard_map/ppermute | solution.py:23
  340.2 9.5 %copy-start.19 = (bf16[32,24,256]{2,1,0:T(8,128)(2,1)}, bf16[32,24,256]{2,1,0:T(8,128)(2,1)S(1)}, u32[]{:S(2)}) copy-start(bf16[32,24,256]{2,1,0:T(8,128)(2,1)S(1)} %get-tuple-element.44) | copy-start | bytes 1179652
  340.2 9.6 %copy-start.21 = (bf16[32,24,256]{2,1,0:T(8,128)(2,1)}, bf16[32,24,256]{2,1,0:T(8,128)(2,1)S(1)}, u32[]{:S(2)}) copy-start(bf16[32,24,256]{2,1,0:T(8,128)(2,1)S(1)} %get-tuple-element.45) | copy-start | bytes 1179652
  360.6 178.2 %reduce-scatter.5.cloned.1.call-start = ((), (), s32[]{:S(2)}) async-start(), calls=%async_computation.3 | async-start | bytes 663552 | tf_op jit(solution)/shard_map/reduce_scatter | solution.py:112
  362.1 5.1 copy-start.22
  362.1 10.1 %slice-start = ((s8[9437184]{0:T(1024)(128)(4,1)}), s8[4194304]{0:T(1024)(128)(4,1)S(1)}, s32[]{:S(2)}) async-start(s8[9437184]{0:T(1024)(128)(4,1)} %bitcast.131), calls=%async_computation.4 | async-start | bytes 8388608
  362.2 10.1 %slice-start.1 = ((s8[9437184]{0:T(1024)(128)(4,1)}), s8[4194304]{0:T(1024)(128)(4,1)S(1)}, s32[]{:S(2)}) async-start(s8[9437184]{0:T(1024)(128)(4,1)} %bitcast.131), calls=%async_computation.5 | async-start | bytes 8388608
  367.2 5.0 slice-start.2
  367.2 5.0 copy-start.20
  372.3 3.7 copy-start.18
  379.6 3.6 copy-start.14
  383.2 3.7 copy-start.12
  386.9 3.6 copy-start.10
  390.6 78.0 %copy-start.24 = (bf16[32,24,256]{2,1,0:T(8,128)(2,1)S(1)}, bf16[32,24,256]{2,1,0:T(8,128)(2,1)}, u32[]{:S(2)}) copy-start(bf16[32,24,256]{2,1,0:T(8,128)(2,1)} %copy-done.23) | copy-start | bytes 1179652
  468.6 71.8 %copy-start.1 = (f32[3,256]{1,0:T(4,128)S(1)}, f32[3,256]{1,0:T(4,128)}, u32[]{:S(2)}) copy-start(f32[3,256]{1,0:T(4,128)} %param.10) | copy-start | bytes 9220
  (17 other events, 32.9 us)
Sparse Core Ops, SparseCore 0:
  360.8 107.7 reduce-scatter.2
  472.1 66.6 reduce-scatter.4
